TPU v7x, 32 devices: a whole 2x2x4 slice. The times are simulated.
32 devices in a mesh: groups: 2 (over y), seq: 8 (over z, x), head: 2 (over core).
Axes of the slice: x: 2, y: 2, z: 4, core: 2. Of those that a mesh axis runs over, the one named last changes fastest.
Arguments:
- queries: bfloat16 [4096, 4096], P(('groups', 'seq'), 'head'), parts along dimension 0, may hold values from -40 to 40
- key_vectors: bfloat16 [4096, 4096], P(('groups', 'seq'), 'head'), parts along dimension 0, may hold values from -6 to 6
- value_vectors: bfloat16 [4096, 4096], P(('groups', 'seq'), 'head'), parts along dimension 0, may hold values from -40 to 40
- output_grad: bfloat16 [4096, 4096], P(('groups', 'seq'), 'head'), parts along dimension 0, may hold values from -6 to 6
- norm_gain: float32 [4096], P('head'), may hold values from 0.5 to 2
- block_docs: int32 [16], P(('groups', 'seq')), parts along dimension 0, may hold values from 0 to 3, never falling along the last dimension, each value on 1 to 4 neighbouring positions
Outputs:
- normed: bfloat16 [4096, 4096], P(('groups', 'seq'), 'head'), parts along dimension 0
- query_grad: bfloat16 [4096, 4096], P(('groups', 'seq'), 'head'), parts along dimension 0
- key_grad: bfloat16 [4096, 4096], P(('groups', 'seq'), 'head'), parts along dimension 0
- value_grad: bfloat16 [4096, 4096], P(('groups', 'seq'), 'head'), parts along dimension 0
There are 2 independent parts, one for each index of `groups`. A program takes and returns all parts, laid end to end along the dimension named above; an argument that names none is the same for every part. Nothing has to cross between parts.
Inputs may be any that keep to these rules, and one draw needn't show every extreme that they name: `block_docs`: block document ids never fall along the sequence; every one of the 4 documents covers 1 to 4 blocks, and one covers exactly 4.
All inputs are finite; a program needn't handle non-finite values.
Results may differ from a plain program's by a relative error of at most 0.0058.
Values sent between devices are 32-bit elements; how exact they have to be, the bound alone decides.
No kernel may reach another device: no remote copies, remote signals or barrier semaphores. Data moves between devices by JAX's collectives and lax.ppermute only.
A program may use at most 64 MiB of HBM per device.

v0:
```python
import jax
import jax.numpy as jnp
from jax import lax
from jax.sharding import PartitionSpec as P

HEAD_DIM = 128
norm_eps = 1e-06


def spread_prefix(element, weights):
    seq_count = lax.axis_size("seq")
    flat_state = element.reshape(seq_count, -1, element.shape[-1])
    mixed = jnp.einsum(
        "ds,skc->dkc",
        weights,
        lax.all_to_all(flat_state, "seq", split_axis=0, concat_axis=0, tiled=True),
        precision=lax.Precision.HIGHEST,
    )
    returned = lax.all_to_all(mixed, "seq", split_axis=0, concat_axis=0, tiled=True)
    return returned.reshape(element.shape)


def body(queries, key_vectors, value_vectors, output_grad, norm_gain, block_docs):
    tokens, local_width = queries.shape
    heads_here = local_width // HEAD_DIM
    nblocks = block_docs.shape[0]
    block_len = tokens // nblocks
    shape_four = (nblocks, block_len, heads_here, HEAD_DIM)
    query_blk = queries.reshape(shape_four)
    key_blk = key_vectors.reshape(shape_four)
    value_blk = value_vectors.reshape(shape_four)
    tok_pos = lax.iota(jnp.int32, block_len)
    causal = (tok_pos[:, None] >= tok_pos[None, :])[None, None]
    scores = jnp.einsum("bthd,bshd->bhts", query_blk, key_blk, preferred_element_type=jnp.float32)
    att_weights = jnp.where(causal, scores, 0.0).astype(jnp.bfloat16)
    intra_out = jnp.einsum(
        "bhts,bshe->bthe", att_weights, value_blk, preferred_element_type=jnp.float32
    )
    block_kv = jnp.einsum("bshd,bshe->bhde", key_blk, value_blk, preferred_element_type=jnp.float32)
    position = lax.iota(jnp.int32, nblocks)
    same_doc = block_docs[:, None] == block_docs[None, :]
    earlier_mask = (same_doc & (position[None, :] < position[:, None])).astype(jnp.float32)
    later_mask = (same_doc & (position[None, :] > position[:, None])).astype(jnp.float32)
    local_in = jnp.einsum("kj,jhde->khde", earlier_mask, block_kv, precision=lax.Precision.HIGHEST)
    tail_weight = (block_docs == block_docs[-1]).astype(jnp.float32)
    tail_state = jnp.einsum("j,jhde->hde", tail_weight, block_kv, precision=lax.Precision.HIGHEST)
    seq_count = lax.axis_size("seq")
    all_docs = lax.all_gather(block_docs, "seq", axis=0, tiled=True).reshape(seq_count, nblocks)
    first_all = all_docs[:, 0]
    last_all = all_docs[:, -1]
    source_pos = lax.iota(jnp.int32, seq_count)
    forward_weights = (
        (source_pos[None, :] < source_pos[:, None]) & (last_all[None, :] == first_all[:, None])
    ).astype(jnp.float32)
    backward_weights = (
        (source_pos[None, :] > source_pos[:, None]) & (first_all[None, :] == last_all[:, None])
    ).astype(jnp.float32)
    carry_state = spread_prefix(tail_state, forward_weights)
    carry_use = block_docs == block_docs[0]
    states_in = (
        local_in + jnp.where(carry_use[:, None, None, None], carry_state[None], 0.0)
    ).astype(jnp.bfloat16)
    inter_out = jnp.einsum(
        "bthd,bhde->bthe", query_blk, states_in, preferred_element_type=jnp.float32
    )
    attended = (intra_out + inter_out).reshape(tokens, local_width)
    scaled_grad = norm_gain[None, :] * output_grad.astype(jnp.float32)
    square_sum, cross_sum = lax.psum(
        (jnp.sum(attended * attended, axis=1), jnp.sum(attended * scaled_grad, axis=1)), "head"
    )
    full_width = local_width * lax.axis_size("head")
    inverse_rms = lax.rsqrt(square_sum / full_width + norm_eps)
    normed = (attended * inverse_rms[:, None] * norm_gain[None, :]).astype(jnp.bfloat16)
    attended_grad = (
        inverse_rms[:, None] * scaled_grad
        - attended * (inverse_rms**3 * cross_sum / full_width)[:, None]
    )
    grad_blk = attended_grad.astype(jnp.bfloat16).reshape(shape_four)
    score_grad = jnp.einsum(
        "bthe,bshe->bhts", grad_blk, value_blk, preferred_element_type=jnp.float32
    )
    grad_weights = jnp.where(causal, score_grad, 0.0).astype(jnp.bfloat16)
    query_part = jnp.einsum(
        "bhts,bshd->bthd", grad_weights, key_blk, preferred_element_type=jnp.float32
    )
    query_part = query_part + jnp.einsum(
        "bthe,bhde->bthd", grad_blk, states_in, preferred_element_type=jnp.float32
    )
    key_intra = jnp.einsum(
        "bhts,bthd->bshd", grad_weights, query_blk, preferred_element_type=jnp.float32
    )
    value_intra = jnp.einsum(
        "bhts,bthe->bshe", att_weights, grad_blk, preferred_element_type=jnp.float32
    )
    block_grad = jnp.einsum(
        "bthd,bthe->bhde", query_blk, grad_blk, preferred_element_type=jnp.float32
    )
    grad_local = jnp.einsum(
        "kj,jhde->khde", later_mask, block_grad, precision=lax.Precision.HIGHEST
    )
    head_weight = (block_docs == block_docs[0]).astype(jnp.float32)
    head_state = jnp.einsum("j,jhde->hde", head_weight, block_grad, precision=lax.Precision.HIGHEST)
    grad_state = spread_prefix(head_state, backward_weights)
    grad_use = block_docs == block_docs[-1]
    grads_in = (
        grad_local + jnp.where(grad_use[:, None, None, None], grad_state[None], 0.0)
    ).astype(jnp.bfloat16)
    key_part = key_intra + jnp.einsum(
        "bshe,bhde->bshd", value_blk, grads_in, preferred_element_type=jnp.float32
    )
    value_part = value_intra + jnp.einsum(
        "bshd,bhde->bshe", key_blk, grads_in, preferred_element_type=jnp.float32
    )
    flat_shape = (tokens, local_width)
    return (
        normed,
        query_part.reshape(flat_shape).astype(jnp.bfloat16),
        key_part.reshape(flat_shape).astype(jnp.bfloat16),
        value_part.reshape(flat_shape).astype(jnp.bfloat16),
    )


def solution(mesh):
    in_specs = (
        P(("groups", "seq"), "head"),
        P(("groups", "seq"), "head"),
        P(("groups", "seq"), "head"),
        P(("groups", "seq"), "head"),
        P("head"),
        P(("groups", "seq")),
    )
    out_specs = (
        P(("groups", "seq"), "head"),
        P(("groups", "seq"), "head"),
        P(("groups", "seq"), "head"),
        P(("groups", "seq"), "head"),
    )
    return jax.shard_map(body, mesh=mesh, in_specs=in_specs, out_specs=out_specs, check_vma=False)
```

profile of v0, /device:TPU:0, one launch (start us, length us, event | category | flops | bytes accessed | tf_op | source)
XLA Modules:
  0.0 156.2 jit_solution(16867197169526272815)
XLA Ops:
  0.6 1.5 copy.72
  4.4 7.3 %all-to-all-start = ((f32[8,256,128]{2,1,0:T(8,128)}), f32[8,256,128]{2,1,0:T(8,128)S(1)}, u32[]{:S(2)}, u32[]{:S(2)}) async-start(f32[8,256,128]{2,1,0:T(8,128)} %bitcast.3), calls=%async_computation | async-start | bytes 2097152 | tf_op jit(solution)/shard_map/all_to_all | solution.py:16
  13.7 23.9 %all-reduce = s32[8]{0:T(128)S(1)} all-reduce(s32[8]{0:T(128)S(1)} %dynamic-update-slice), channel_id=1, replica_groups=mesh['groups'=2,'seq'=8,'head'=2] {'seq'}, use_global_device_ids=true, to_apply=%add | all-reduce | flops 8 | bytes 64
  40.0 3.6 %all-to-all-start.1 = ((f32[8,256,128]{2,1,0:T(8,128)}), f32[8,256,128]{2,1,0:T(8,128)S(1)}, u32[]{:S(2)}, u32[]{:S(2)}) async-start(f32[8,256,128]{2,1,0:T(8,128)} %copy.44), calls=%async_computation.1 | async-start | bytes 2097152 | tf_op jit(solution)/shard_map/all_to_all | solution.py:19
  43.6 1.5 copy.68
  45.1 2.4 %select_convert_fusion.1 = bf16[16,256,256]{2,1,0:T(8,128)(2,1)S(1)} fusion(bf16[256,16,128]{0,2,1:T(8,128)(2,1)S(1)} %bitcast.111, pred[256,256]{1,0:T(8,128)(4,1)S(1)} %iota_compare_fusion, bf16[256,2048]{1,0:T(8,128)(2,1)} %param.7), kind=kOutput, calls=%fused_computation.1 | convolution fusion | flops 270532608 | bytes 4259840 | tf_op jit(solution)/shard_map/bthd,bshd->bhts/dot_general | solution.py:34
  48.8 2.2 %fusion.3 = f32[16,256,128]{1,2,0:T(8,128)} fusion(bf16[16,256,256]{2,1,0:T(8,128)(2,1)S(1)} %select_convert_fusion.1, bf16[256,2048]{1,0:T(8,128)(2,1)S(1)} %copy-done), kind=kOutput, calls=%fused_computation.14 | convolution fusion | flops 268435456 | bytes 5242880 | tf_op jit(solution)/shard_map/bhts,bshe->bthe/dot_general | solution.py:36
  50.9 18.6 %all-to-all-done.1 = f32[8,256,128]{2,1,0:T(8,128)S(1)} async-done(((f32[8,256,128]{2,1,0:T(8,128)}), f32[8,256,128]{2,1,0:T(8,128)S(1)}, u32[]{:S(2)}, u32[]{:S(2)}) %all-to-all-start.1) | async-done | bytes 1048608 | tf_op jit(solution)/shard_map/all_to_all | solution.py:19
  69.5 1.5 add_convert_fusion.1
  71.4 1.8 %fusion.2 = (f32[256]{0:T(256)S(1)}, f32[16,128,256]{2,1,0:T(8,128)}) fusion(bf16[16,128,128]{2,1,0:T(8,128)(2,1)S(1)} %add_convert_fusion.1, bf16[256,16,128]{0,2,1:T(8,128)(2,1)S(1)} %bitcast.112, f32[16,256,128]{1,2,0:T(8,128)S(1)} %copy-done.7), kind=kOutput, calls=%fused_computation.7 | convolution fusion | flops 135790336 | bytes 5768192 | tf_op jit(solution)/shard_map/bthd,bhde->bthe/dot_general | solution.py:63
  73.3 1.9 %copy.47 = f32[256,2048]{1,0:T(8,128)S(1)} copy(f32[256,2048]{0,1:T(8,128)} %bitcast.116) | data formatting | bytes 4194304 | tf_op jit(solution)/shard_map/reshape | solution.py:66
  75.2 1.6 %multiply_reduce_fusion = f32[256]{0:T(256)S(1)} fusion(f32[256,2048]{1,0:T(8,128)S(1)} %copy.47, bf16[256,2048]{1,0:T(8,128)(2,1)} %param.9, f32[2048]{0:T(1024)S(1)} %copy-done.13), kind=kLoop, calls=%fused_computation.11 | loop fusion | flops 2096896 | bytes 3154944 | tf_op jit(solution)/shard_map/reduce_sum | solution.py:69
  76.8 2.5 %all-reduce.1 = (f32[256]{0:T(256)S(1)}, f32[256]{0:T(256)S(1)}) all-reduce(f32[256]{0:T(256)S(1)} %get-tuple-element.18, f32[256]{0:T(256)S(1)} %multiply_reduce_fusion), channel_id=1, replica_groups=mesh['groups'=2,'seq'=8,'head'=2] {'head'}, use_global_device_ids=true, to_apply=%region_1.2 | all-reduce | flops 512 | bytes 4096 | tf_op jit(solution)/shard_map/psum | solution.py:68
  79.3 3.6 %subtract_convert_fusion = (bf16[256,2048]{1,0:T(8,128)(2,1)}, bf16[256,2048]{1,0:T(8,128)(2,1)}) fusion(f32[256,2048]{1,0:T(8,128)S(1)} %copy.47, bf16[256,2048]{1,0:T(8,128)(2,1)} %param.9, f32[256]{0:T(256)S(1)} %get-tuple-element.16, f32[2048]{0:T(1024)S(1)} %copy-done.13, f32[256]{0:T(256)S(1)} %get-tuple-element.17), kind=kLoop, calls=%fused_computation.10 | loop fusion | flops 4718592 | bytes 5253120 | tf_op jit(solution)/shard_map/convert_element_type | solution.py:78
  82.8 1.6 %copy.69 = bf16[256,2048]{0,1:T(8,128)(2,1)S(1)} copy(bf16[256,2048]{1,0:T(8,128)(2,1)} %get-tuple-element.14) | data formatting | bytes 2097152 | tf_op jit(solution)/shard_map/reshape.36
  84.9 29.5 %all_to_all.20 = f32[8,256,128]{2,1,0:T(8,128)S(1)} all-to-all(f32[8,256,128]{2,1,0:T(8,128)S(1)} %bitcast.115), channel_id=1, replica_groups=mesh['groups'=2,'seq'=8,'head'=2] {'seq'}, dimensions={0} | all-to-all | bytes 2097152 | tf_op jit(solution)/shard_map/all_to_all | solution.py:16
  116.7 4.4 %all-to-all-start.3 = ((f32[8,256,128]{2,1,0:T(8,128)}), f32[8,256,128]{2,1,0:T(8,128)}, u32[]{:S(2)}, u32[]{:S(2)}) async-start(f32[8,256,128]{2,1,0:T(8,128)} %copy.58), calls=%async_computation.3 | async-start | bytes 2097152 | tf_op jit(solution)/shard_map/all_to_all | solution.py:19
  123.8 1.4 fusion.1
  125.2 2.3 %copy.63 = bf16[256,2048]{1,0:T(8,128)(2,1)} copy(bf16[256,2048]{0,1:T(8,128)(2,1)} %bitcast.121) | data formatting | bytes 2097152
  127.5 3.4 %fusion.35 = f32[16,128,256]{2,1,0:T(8,128)} fusion(bf16[256,16,128]{0,2,1:T(8,128)(2,1)S(1)} %bitcast.110, bf16[16,256,256]{2,1,0:T(8,128)(2,1)} %copy-done.8), kind=kOutput, calls=%fused_computation.53 | convolution fusion | flops 268435456 | bytes 5242880 | tf_op jit(solution)/shard_map/bhts,bthe->bshe/dot_general | solution.py:92
  130.8 15.1 %all-to-all-done.3 = f32[8,256,128]{2,1,0:T(8,128)} async-done(((f32[8,256,128]{2,1,0:T(8,128)}), f32[8,256,128]{2,1,0:T(8,128)}, u32[]{:S(2)}, u32[]{:S(2)}) %all-to-all-start.3) | async-done | bytes 1048608 | tf_op jit(solution)/shard_map/all_to_all | solution.py:19
  145.9 1.7 %fusion.13 = bf16[16,128,128]{2,1,0:T(8,128)(2,1)S(1)} fusion(f32[16,128,128]{2,1,0:T(8,128)} %bitcast.18, f32[16,128,128]{1,2,0:T(8,128)} %copy-done.5), kind=kLoop, calls=%fused_computation.25 | loop fusion | flops 786432 | bytes 2621440 | tf_op jit(solution)/shard_map/convert_element_type | solution.py:107
  147.6 1.8 %fusion.5 = f32[16,128,256]{2,1,0:T(8,128)} fusion(bf16[16,128,128]{2,1,0:T(8,128)(2,1)S(1)} %fusion.13, bf16[256,2048]{1,0:T(8,128)(2,1)S(1)} %copy-done), kind=kOutput, calls=%fused_computation.16 | convolution fusion | flops 134217728 | bytes 3670016 | tf_op jit(solution)/shard_map/bshe,bhde->bshd/dot_general | solution.py:108
  152.1 2.7 %fusion = bf16[16,128,256]{2,1,0:T(8,128)(2,1)S(1)} fusion(f32[16,128,256]{2,1,0:T(8,128)} %fusion.5, bf16[256,16,128]{0,2,1:T(8,128)(2,1)S(1)} %bitcast.114, bf16[16,256,256]{2,1,0:T(8,128)(2,1)} %copy-done.6), kind=kOutput, calls=%fused_computation.3 | convolution fusion | flops 269484032 | bytes 6291456 | tf_op jit(solution)/shard_map/bhts,bthd->bshd/dot_general | solution.py:89
  (48 shorter events, 17.2 us)
Async XLA Ops:
  0.6 2.4 %copy-start = (bf16[256,2048]{1,0:T(8,128)(2,1)S(1)}, bf16[256,2048]{1,0:T(8,128)(2,1)}, u32[]{:S(2)}) copy-start(bf16[256,2048]{1,0:T(8,128)(2,1)} %param.8) | copy-start | bytes 3145732
  3.0 1.4 copy-start.3
  3.0 9.3 %copy-start.14 = (u32[32]{0:T(128)S(1)}, u32[32]{0:T(128)}, u32[]{:S(2)}) copy-start(u32[32]{0:T(128)} %constant.19) | copy-start | bytes 388
  4.4 33.2 %all-to-all-start = ((f32[8,256,128]{2,1,0:T(8,128)}), f32[8,256,128]{2,1,0:T(8,128)S(1)}, u32[]{:S(2)}, u32[]{:S(2)}) async-start(f32[8,256,128]{2,1,0:T(8,128)} %bitcast.3), calls=%async_computation | async-start | bytes 2097152 | tf_op jit(solution)/shard_map/all_to_all | solution.py:16
  40.0 29.5 %all-to-all-start.1 = ((f32[8,256,128]{2,1,0:T(8,128)}), f32[8,256,128]{2,1,0:T(8,128)S(1)}, u32[]{:S(2)}, u32[]{:S(2)}) async-start(f32[8,256,128]{2,1,0:T(8,128)} %copy.44), calls=%async_computation.1 | async-start | bytes 2097152 | tf_op jit(solution)/shard_map/all_to_all | solution.py:19
  45.0 26.0 %copy-start.1 = (bf16[256,2048]{0,1:T(8,128)(2,1)}, bf16[256,2048]{0,1:T(8,128)(2,1)S(1)}, u32[]{:S(2)}) copy-start(bf16[256,2048]{0,1:T(8,128)(2,1)S(1)} %copy.68) | copy-start | bytes 3145732
  47.5 1.3 copy-start.8
  69.5 1.9 %copy-start.7 = (f32[16,256,128]{1,2,0:T(8,128)S(1)}, f32[16,256,128]{1,2,0:T(8,128)}, u32[]{:S(2)}) copy-start(f32[16,256,128]{1,2,0:T(8,128)} %fusion.3) | copy-start | bytes 6291460
  71.4 1.8 %copy-start.10 = (bf16[16,128,128]{2,1,0:T(8,128)(2,1)}, bf16[16,128,128]{2,1,0:T(8,128)(2,1)S(1)}, u32[]{:S(2)}) copy-start(bf16[16,128,128]{2,1,0:T(8,128)(2,1)S(1)} %add_convert_fusion.1) | copy-start | bytes 1572868
  73.3 1.9 %copy-start.13 = (f32[2048]{0:T(1024)S(1)}, f32[2048]{0:T(1024)}, u32[]{:S(2)}) copy-start(f32[2048]{0:T(1024)} %param.10) | copy-start | bytes 24580
  82.8 1.6 %copy-start.2 = (bf16[256,2048]{0,1:T(8,128)(2,1)S(1)}, bf16[256,2048]{0,1:T(8,128)(2,1)}, u32[]{:S(2)}) copy-start(bf16[256,2048]{0,1:T(8,128)(2,1)} %copy-done.1) | copy-start | bytes 3145732
  84.9 30.7 %copy-start.5 = (f32[16,128,128]{1,2,0:T(8,128)}, f32[16,128,128]{1,2,0:T(8,128)S(1)}, u32[]{:S(2)}) copy-start(f32[16,128,128]{1,2,0:T(8,128)S(1)} %fusion.36) | copy-start | bytes 3145732
  116.7 29.2 %all-to-all-start.3 = ((f32[8,256,128]{2,1,0:T(8,128)}), f32[8,256,128]{2,1,0:T(8,128)}, u32[]{:S(2)}, u32[]{:S(2)}) async-start(f32[8,256,128]{2,1,0:T(8,128)} %copy.58), calls=%async_computation.3 | async-start | bytes 2097152 | tf_op jit(solution)/shard_map/all_to_all | solution.py:19
  121.1 1.2 copy-start.4
  122.4 1.3 copy-start.6
  122.4 1.4 copy-start.11
  147.6 1.9 %copy-start.9 = (f32[16,128,256]{2,1,0:T(8,128)S(1)}, f32[16,128,256]{2,1,0:T(8,128)}, u32[]{:S(2)}) copy-start(f32[16,128,256]{2,1,0:T(8,128)} %fusion.35) | copy-start | bytes 6291460
  147.6 2.6 %copy-start.12 = (bf16[256,2048]{1,0:T(8,128)(2,1)S(1)}, bf16[256,2048]{1,0:T(8,128)(2,1)}, u32[]{:S(2)}) copy-start(bf16[256,2048]{1,0:T(8,128)(2,1)} %param.7) | copy-start | bytes 3145732
where the time goes:
time: 157 us; the launch traced here: 156 us
  blocking collectives  55.9 us (36%)
  waiting for transfers between devices  33.7 us (21%)
  matrix products  21.8 us (14%)
  local copies, waits for them, and re-layouts  19.7 us (13%)
  starting transfers between devices  15.3 us (10%)
  other arithmetic  8.37 us (5%)
    all_to_all x2, waiting for transfers between devices, spread_prefix(): lax.all_to_all(mixed, 'seq', split_axis=0, concat_axis=0, tiled=True)  33.7 us
    all_to_all x1, blocking collectives, spread_prefix(): lax.all_to_all(flat_state, 'seq', split_axis=0, concat_axis=0, tiled=True)  29.5 us
    unnamed x1, blocking collectives  23.9 us
    unnamed x37, local copies, waits for them, and re-layouts  11.6 us
    all_to_all x2, starting transfers between devices, spread_prefix(): lax.all_to_all(mixed, 'seq', split_axis=0, concat_axis=0, tiled=True)  8.01 us
    all_to_all x1, starting transfers between devices, spread_prefix(): lax.all_to_all(flat_state, 'seq', split_axis=0, concat_axis=0, tiled=True)  7.25 us
    another operation x3, local copies, waits for them, and re-layouts  3.83 us
    convert_element_type x1, other arithmetic, body(): grad_blk = attended_grad.astype(jnp.bfloat16).reshape(shape_four)  3.57 us
  transfers between devices with their start and end apart: 3, of which 2 were waited for; matrix products, arithmetic and copies ran while one was open for 10% of the time, Pallas kernels for 0%

commit v1 on v0

--- a/solution.py
+++ b/solution.py
@@ -5,6 +5,22 @@
 
 HEAD_DIM = 128
 norm_eps = 1e-06
+
+
+def swapped_with_each(x, axis, split, join):
+    ways, here = (lax.axis_size(axis), lax.axis_index(axis))
+    width = x.shape[split] // ways
+    shape = list(x.shape)
+    shape[split] = width
+    height = shape[join]
+    shape[join] = height * ways
+    full = jnp.zeros(shape, x.dtype)
+    for mask in range(ways):
+        part = lax.dynamic_slice_in_dim(x, (here ^ mask) * width, width, axis=split)
+        if mask:
+            part = lax.ppermute(part, axis, [(d, d ^ mask) for d in range(ways)])
+        full = lax.dynamic_update_slice_in_dim(full, part, (here ^ mask) * height, axis=join)
+    return full
 
 
 def spread_prefix(element, weights):
@@ -16,7 +32,7 @@
         lax.all_to_all(flat_state, "seq", split_axis=0, concat_axis=0, tiled=True),
         precision=lax.Precision.HIGHEST,
     )
-    returned = lax.all_to_all(mixed, "seq", split_axis=0, concat_axis=0, tiled=True)
+    returned = swapped_with_each(mixed, "seq", 0, 0)
     return returned.reshape(element.shape)
 
 

time: 157 us -> 163 us (1.038)
  blocking collectives: 55.9 us -> 26.4 us
  starting transfers between devices: 15.3 us -> 34.7 us
  waiting for transfers between devices: 33.7 us -> 48.7 us
  matrix products: 21.8 us -> 24 us
  other arithmetic: 8.37 us -> 6.69 us
    all_to_all x2 -> x0, waiting for transfers between devices: 33.7 us -> none  [spread_prefix(): lax.all_to_all(mixed, 'seq', split_axis=0, concat_axis=0, tiled=True)]
    all_to_all x1 -> x0, blocking collectives: 29.5 us -> none  [spread_prefix(): lax.all_to_all(flat_state, 'seq', split_axis=0, concat_axis=0, tiled=True)]
    ppermute x0 -> x14, waiting for transfers between devices: none -> 27.4 us  [swapped_with_each(): part = lax.ppermute(part, axis, [(d, d ^ mask) for d in range(ways)])]
    all_to_all x1 -> x2, waiting for transfers between devices: 0.01 us -> 21.4 us  [spread_prefix(): lax.all_to_all(flat_state, 'seq', split_axis=0, concat_axis=0, tiled=True)]
    ppermute x0 -> x14, starting transfers between devices: none -> 21.2 us  [swapped_with_each(): part = lax.ppermute(part, axis, [(d, d ^ mask) for d in range(ways)])]
    all_to_all x2 -> x0, starting transfers between devices: 8.01 us -> none  [spread_prefix(): lax.all_to_all(mixed, 'seq', split_axis=0, concat_axis=0, tiled=True)]
    all_to_all x1 -> x2, starting transfers between devices: 7.25 us -> 13.5 us  [spread_prefix(): lax.all_to_all(flat_state, 'seq', split_axis=0, concat_axis=0, tiled=True)]
    dot_general x2 -> x0, local copies, waits for them, and re-layouts: 2.32 us -> none  [spread_prefix(): jnp.einsum('ds,skc->dkc', weights, lax.all_to_all(flat_state, 'seq', spli...]
  transfers between devices with their start and end apart: 3 -> 16, of which waited for: 2 -> 6; matrix products, arithmetic and copies ran while one was open for 10% -> 11% of each run, Pallas kernels for 0% -> 0%
where the time goes in v1:
time: 163 us; the launch traced here: 162 us
  waiting for transfers between devices  48.7 us (30%)
  starting transfers between devices  34.7 us (21%)
  blocking collectives  26.4 us (16%)
  matrix products  24 us (15%)
  local copies, waits for them, and re-layouts  19.3 us (12%)
  other arithmetic  6.69 us (4%)
  between operations  1.77 us (1%)
    ppermute x14, waiting for transfers between devices, swapped_with_each(): part = lax.ppermute(part, axis, [(d, d ^ mask) for d in range(ways)])  27.4 us
    unnamed x1, blocking collectives  23.9 us
    all_to_all x2, waiting for transfers between devices, spread_prefix(): lax.all_to_all(flat_state, 'seq', split_axis=0, concat_axis=0, tiled=True)  21.4 us
    ppermute x14, starting transfers between devices, swapped_with_each(): part = lax.ppermute(part, axis, [(d, d ^ mask) for d in range(ways)])  21.2 us
    all_to_all x2, starting transfers between devices, spread_prefix(): lax.all_to_all(flat_state, 'seq', split_axis=0, concat_axis=0, tiled=True)  13.5 us
    unnamed x47, local copies, waits for them, and re-layouts  9.97 us
    another operation x5, local copies, waits for them, and re-layouts  3.96 us
    dot_general x2, matrix products, spread_prefix(): jnp.einsum('ds,skc->dkc', weights, lax.all_to_all(flat_state, 'seq', spli...  3.71 us
  transfers between devices with their start and end apart: 16, of which 6 were waited for; matrix products, arithmetic and copies ran while one was open for 11% of the time, Pallas kernels for 0%

profile of v1, /device:TPU:0, one launch (start us, length us, event | category | flops | bytes accessed | tf_op | source)
XLA Modules:
  0.0 161.6 jit_solution(2606163807864282826)
XLA Ops:
  4.4 7.3 %all-to-all-start = ((f32[8,256,128]{2,1,0:T(8,128)}), f32[8,256,128]{2,1,0:T(8,128)S(1)}, u32[]{:S(2)}, u32[]{:S(2)}) async-start(f32[8,256,128]{2,1,0:T(8,128)} %bitcast.3), calls=%async_computation | async-start | bytes 2097152 | tf_op jit(solution)/shard_map/all_to_all | solution.py:32
  13.7 23.9 %all-reduce = s32[8]{0:T(128)S(1)} all-reduce(s32[8]{0:T(128)S(1)} %dynamic-update-slice), channel_id=1, replica_groups=mesh['groups'=2,'seq'=8,'head'=2] {'seq'}, use_global_device_ids=true, to_apply=%add | all-reduce | flops 8 | bytes 64
  39.2 3.7 %select_convert_fusion.1 = bf16[16,256,256]{2,1,0:T(8,128)(2,1)} fusion(bf16[256,16,128]{0,2,1:T(8,128)(2,1)S(1)} %bitcast.127, pred[256,256]{1,0:T(8,128)(4,1)S(1)} %iota_compare_fusion, bf16[256,2048]{1,0:T(8,128)(2,1)} %param.7), kind=kOutput, calls=%fused_computation.1 | convolution fusion | flops 270532608 | bytes 4259840 | tf_op jit(solution)/shard_map/bthd,bshd->bhts/dot_general | solution.py:50
  47.2 2.1 %collective-permute-start.2 = (f32[1,256,128]{2,0,1:T(1,128)S(1)}, f32[1,256,128]{2,0,1:T(1,128)S(1)}, u32[]{:S(2)}, u32[]{:S(2)}) collective-permute-start(f32[1,256,128]{2,0,1:T(1,128)S(1)} %get-tuple-element.28), channel_id=1, source_target_pairs={{0,6},{2,4},{4,2},{6,0},{8,14},{10,12},{12,10},{14,8},{1,7},{3,5},... | collective-permute-start | bytes 393224 | tf_op jit(solution)/shard_map/ppermute | solution.py:21
  49.3 3.8 %collective-permute-start.4 = (f32[1,256,128]{2,0,1:T(1,128)S(1)}, f32[1,256,128]{2,0,1:T(1,128)S(1)}, u32[]{:S(2)}, u32[]{:S(2)}) collective-permute-start(f32[1,256,128]{2,0,1:T(1,128)S(1)} %get-tuple-element.26), channel_id=1, source_target_pairs={{0,10},{2,8},{4,14},{6,12},{8,2},{10,0},{12,6},{14,4},{1,11},{3,9}... | collective-permute-start | bytes 393224 | tf_op jit(solution)/shard_map/ppermute | solution.py:21
  57.2 10.6 %collective-permute-done.3 = f32[1,256,128]{2,0,1:T(1,128)S(1)} collective-permute-done((f32[1,256,128]{2,0,1:T(1,128)S(1)}, f32[1,256,128]{2,0,1:T(1,128)S(1)}, u32[]{:S(2)}, u32[]{:S(2)}) %collective-permute-start.3) | collective-permute-done | bytes 131104 | tf_op jit(solution)/shard_map/ppermute | solution.py:21
  67.8 3.0 %collective-permute-done.4 = f32[1,256,128]{2,0,1:T(1,128)S(1)} collective-permute-done((f32[1,256,128]{2,0,1:T(1,128)S(1)}, f32[1,256,128]{2,0,1:T(1,128)S(1)}, u32[]{:S(2)}, u32[]{:S(2)}) %collective-permute-start.4) | collective-permute-done | bytes 131104 | tf_op jit(solution)/shard_map/ppermute | solution.py:21
  72.3 1.9 %fusion.2 = (f32[256]{0:T(256)S(1)}, f32[16,128,256]{2,1,0:T(8,128)}) fusion(bf16[16,128,128]{2,1,0:T(8,128)(2,1)S(1)} %add_convert_fusion.1, bf16[256,16,128]{0,2,1:T(8,128)(2,1)S(1)} %bitcast.128, f32[16,256,128]{1,2,0:T(8,128)S(1)} %fusion.3), kind=kOutput, calls=%fused_computation.7 | convolution fusion | flops 135790336 | bytes 5768192 | tf_op jit(solution)/shard_map/bthd,bhde->bthe/dot_general | solution.py:79
  74.1 1.9 %copy.68 = f32[256,2048]{1,0:T(8,128)S(1)} copy(f32[256,2048]{0,1:T(8,128)} %bitcast.132) | data formatting | bytes 4194304 | tf_op jit(solution)/shard_map/reshape | solution.py:82
  77.7 2.5 %all-reduce.1 = (f32[256]{0:T(256)S(1)}, f32[256]{0:T(256)S(1)}) all-reduce(f32[256]{0:T(256)S(1)} %get-tuple-element.34, f32[256]{0:T(256)S(1)} %multiply_reduce_fusion), channel_id=1, replica_groups=mesh['groups'=2,'seq'=8,'head'=2] {'head'}, use_global_device_ids=true, to_apply=%region_1.2 | all-reduce | flops 512 | bytes 4096 | tf_op jit(solution)/shard_map/psum | solution.py:84
  80.2 3.6 %subtract_convert_fusion = (bf16[256,2048]{1,0:T(8,128)(2,1)}, bf16[256,2048]{1,0:T(8,128)(2,1)}) fusion(f32[256,2048]{1,0:T(8,128)S(1)} %copy.68, bf16[256,2048]{1,0:T(8,128)(2,1)} %param.9, f32[256]{0:T(256)S(1)} %get-tuple-element.32, f32[2048]{0:T(1024)S(1)} %copy-done.18, f32[256]{0:T(256)S(1)} %get-tuple-element.33), kind=kLoop, calls=%fused_computation.10 | loop fusion | flops 4718592 | bytes 5253120 | tf_op jit(solution)/shard_map/convert_element_type | solution.py:94
  86.7 6.3 %all-to-all-start.1 = ((f32[8,256,128]{2,1,0:T(8,128)}), f32[8,256,128]{2,1,0:T(8,128)}, u32[]{:S(2)}, u32[]{:S(2)}) async-start(f32[8,256,128]{2,1,0:T(8,128)} %bitcast.131), calls=%async_computation.1 | async-start | bytes 2097152 | tf_op jit(solution)/shard_map/all_to_all | solution.py:32
  94.6 1.8 %fusion.35 = f32[16,128,256]{2,1,0:T(8,128)} fusion(bf16[256,16,128]{0,2,1:T(8,128)(2,1)S(1)} %bitcast.125, bf16[16,256,256]{2,1,0:T(8,128)(2,1)S(1)} %copy-done.8), kind=kOutput, calls=%fused_computation.85 | convolution fusion | flops 268435456 | bytes 5242880 | tf_op jit(solution)/shard_map/bhts,bthe->bshe/dot_general | solution.py:108
  96.6 2.2 %fusion.34 = f32[16,256,128]{1,2,0:T(8,128)} fusion(bf16[16,256,256]{2,1,0:T(8,128)(2,1)S(1)} %select_convert_fusion, bf16[256,16,128]{0,2,1:T(8,128)(2,1)S(1)} %copy-done.4), kind=kOutput, calls=%fused_computation.84 | convolution fusion | flops 268435456 | bytes 5242880 | tf_op jit(solution)/shard_map/bhts,bshd->bthd/dot_general | solution.py:99
  98.8 21.4 %all-to-all-done.1 = f32[8,256,128]{2,1,0:T(8,128)} async-done(((f32[8,256,128]{2,1,0:T(8,128)}), f32[8,256,128]{2,1,0:T(8,128)}, u32[]{:S(2)}, u32[]{:S(2)}) %all-to-all-start.1) | async-done | bytes 1048608 | tf_op jit(solution)/shard_map/all_to_all | solution.py:32
  120.2 2.5 %fusion.14 = f32[8,256,128]{2,0,1:T(8,128)S(1)} fusion(f32[8,256,128]{2,1,0:T(8,128)} %all-to-all-done.1, s32[8]{0:T(128)S(1)} %all-reduce), kind=kOutput, calls=%fused_computation.26 | convolution fusion | flops 25166016 | bytes 2097184 | tf_op jit(solution)/shard_map/ds,skc->dkc/dot_general | solution.py:29
  126.1 2.3 %copy.91 = bf16[256,2048]{1,0:T(8,128)(2,1)} copy(bf16[256,2048]{0,1:T(8,128)(2,1)} %bitcast.137) | data formatting | bytes 2097152
  128.5 3.0 %collective-permute-start.9 = (f32[1,256,128]{2,0,1:T(1,128)S(1)}, f32[1,256,128]{2,0,1:T(1,128)S(1)}, u32[]{:S(2)}, u32[]{:S(2)}) collective-permute-start(f32[1,256,128]{2,0,1:T(1,128)S(1)} %copy-done.16), channel_id=1, source_target_pairs={{0,6},{2,4},{4,2},{6,0},{8,14},{10,12},{12,10},{14,8},{1,7},{3,5},... | collective-permute-start | bytes 393224 | tf_op jit(solution)/shard_map/ppermute | solution.py:21
  131.5 2.8 %collective-permute-start.11 = (f32[1,256,128]{2,0,1:T(1,128)S(1)}, f32[1,256,128]{2,0,1:T(1,128)S(1)}, u32[]{:S(2)}, u32[]{:S(2)}) collective-permute-start(f32[1,256,128]{2,0,1:T(1,128)S(1)} %copy-done.14), channel_id=1, source_target_pairs={{0,10},{2,8},{4,14},{6,12},{8,2},{10,0},{12,6},{14,4},{1,11},{3,9}... | collective-permute-start | bytes 393224 | tf_op jit(solution)/shard_map/ppermute | solution.py:21
  136.9 3.4 %collective-permute-start.13 = (f32[1,256,128]{2,0,1:T(1,128)S(1)}, f32[1,256,128]{2,0,1:T(1,128)S(1)}, u32[]{:S(2)}, u32[]{:S(2)}) collective-permute-start(f32[1,256,128]{2,0,1:T(1,128)S(1)} %get-tuple-element.16), channel_id=1, source_target_pairs={{0,14},{2,12},{4,10},{6,8},{8,6},{10,4},{12,2},{14,0},{1,15},{3,13... | collective-permute-start | bytes 393224 | tf_op jit(solution)/shard_map/ppermute | solution.py:21
  140.4 9.3 %collective-permute-done.10 = f32[1,256,128]{2,0,1:T(1,128)S(1)} collective-permute-done((f32[1,256,128]{2,0,1:T(1,128)S(1)}, f32[1,256,128]{2,0,1:T(1,128)S(1)}, u32[]{:S(2)}, u32[]{:S(2)}) %collective-permute-start.10) | collective-permute-done | bytes 131104 | tf_op jit(solution)/shard_map/ppermute | solution.py:21
  149.7 3.0 %collective-permute-done.11 = f32[1,256,128]{2,0,1:T(1,128)S(1)} collective-permute-done((f32[1,256,128]{2,0,1:T(1,128)S(1)}, f32[1,256,128]{2,0,1:T(1,128)S(1)}, u32[]{:S(2)}, u32[]{:S(2)}) %collective-permute-start.11) | collective-permute-done | bytes 131104 | tf_op jit(solution)/shard_map/ppermute | solution.py:21
  152.9 1.8 %fusion.5 = f32[16,128,256]{2,1,0:T(8,128)} fusion(bf16[16,128,128]{2,1,0:T(8,128)(2,1)S(1)} %fusion.13, bf16[256,2048]{1,0:T(8,128)(2,1)S(1)} %copy-done), kind=kOutput, calls=%fused_computation.16 | convolution fusion | flops 134217728 | bytes 3670016 | tf_op jit(solution)/shard_map/bshe,bhde->bshd/dot_general | solution.py:124
  157.5 2.7 %fusion = bf16[16,128,256]{2,1,0:T(8,128)(2,1)S(1)} fusion(f32[16,128,256]{2,1,0:T(8,128)} %fusion.5, bf16[256,16,128]{0,2,1:T(8,128)(2,1)S(1)} %bitcast.130, bf16[16,256,256]{2,1,0:T(8,128)(2,1)} %copy-done.6), kind=kOutput, calls=%fused_computation.3 | convolution fusion | flops 269484032 | bytes 6291456 | tf_op jit(solution)/shard_map/bhts,bthd->bshd/dot_general | solution.py:105
  (101 shorter events, 33.2 us)
Async XLA Ops:
  3.0 9.3 %copy-start.19 = (u32[32]{0:T(128)S(1)}, u32[32]{0:T(128)}, u32[]{:S(2)}) copy-start(u32[32]{0:T(128)} %constant.44) | copy-start | bytes 388
  4.4 38.4 %all-to-all-start = ((f32[8,256,128]{2,1,0:T(8,128)}), f32[8,256,128]{2,1,0:T(8,128)S(1)}, u32[]{:S(2)}, u32[]{:S(2)}) async-start(f32[8,256,128]{2,1,0:T(8,128)} %bitcast.3), calls=%async_computation | async-start | bytes 2097152 | tf_op jit(solution)/shard_map/all_to_all | solution.py:32
  39.1 33.2 %copy-start.1 = (bf16[256,2048]{0,1:T(8,128)(2,1)}, bf16[256,2048]{0,1:T(8,128)(2,1)S(1)}, u32[]{:S(2)}) copy-start(bf16[256,2048]{0,1:T(8,128)(2,1)S(1)} %copy.96) | copy-start | bytes 3145732
  42.9 3.4 %copy-start.7 = (bf16[16,256,256]{2,1,0:T(8,128)(2,1)S(1)}, bf16[16,256,256]{2,1,0:T(8,128)(2,1)}, u32[]{:S(2)}) copy-start(bf16[16,256,256]{2,1,0:T(8,128)(2,1)} %select_convert_fusion.1) | copy-start | bytes 6291460
  44.8 8.4 %collective-permute-start = (f32[1,256,128]{2,0,1:T(1,128)S(1)}, f32[1,256,128]{2,0,1:T(1,128)S(1)}, u32[]{:S(2)}, u32[]{:S(2)}) collective-permute-start(f32[1,256,128]{2,0,1:T(1,128)S(1)} %get-tuple-element.30), channel_id=1, source_target_pairs={{0,2},{2,0},{4,6},{6,4},{8,10},{10,8},{12,14},{14,12},{1,3},{3,1},... | collective-permute-start | bytes 393224 | tf_op jit(solution)/shard_map/ppermute | solution.py:21
  47.1 9.1 %collective-permute-start.1 = (f32[1,256,128]{2,0,1:T(1,128)S(1)}, f32[1,256,128]{2,0,1:T(1,128)S(1)}, u32[]{:S(2)}, u32[]{:S(2)}) collective-permute-start(f32[1,256,128]{2,0,1:T(1,128)S(1)} %get-tuple-element.29), channel_id=1, source_target_pairs={{0,4},{2,6},{4,0},{6,2},{8,12},{10,14},{12,8},{14,10},{1,5},{3,7},... | collective-permute-start | bytes 393224 | tf_op jit(solution)/shard_map/ppermute | solution.py:21
  47.2 10.0 %collective-permute-start.2 = (f32[1,256,128]{2,0,1:T(1,128)S(1)}, f32[1,256,128]{2,0,1:T(1,128)S(1)}, u32[]{:S(2)}, u32[]{:S(2)}) collective-permute-start(f32[1,256,128]{2,0,1:T(1,128)S(1)} %get-tuple-element.28), channel_id=1, source_target_pairs={{0,6},{2,4},{4,2},{6,0},{8,14},{10,12},{12,10},{14,8},{1,7},{3,5},... | collective-permute-start | bytes 393224 | tf_op jit(solution)/shard_map/ppermute | solution.py:21
  49.3 18.5 %collective-permute-start.3 = (f32[1,256,128]{2,0,1:T(1,128)S(1)}, f32[1,256,128]{2,0,1:T(1,128)S(1)}, u32[]{:S(2)}, u32[]{:S(2)}) collective-permute-start(f32[1,256,128]{2,0,1:T(1,128)S(1)} %get-tuple-element.27), channel_id=1, source_target_pairs={{0,8},{2,10},{4,12},{6,14},{8,0},{10,2},{12,4},{14,6},{1,9},{3,11}... | collective-permute-start | bytes 393224 | tf_op jit(solution)/shard_map/ppermute | solution.py:21
  49.3 21.5 %collective-permute-start.4 = (f32[1,256,128]{2,0,1:T(1,128)S(1)}, f32[1,256,128]{2,0,1:T(1,128)S(1)}, u32[]{:S(2)}, u32[]{:S(2)}) collective-permute-start(f32[1,256,128]{2,0,1:T(1,128)S(1)} %get-tuple-element.26), channel_id=1, source_target_pairs={{0,10},{2,8},{4,14},{6,12},{8,2},{10,0},{12,6},{14,4},{1,11},{3,9}... | collective-permute-start | bytes 393224 | tf_op jit(solution)/shard_map/ppermute | solution.py:21
  53.2 17.7 %collective-permute-start.5 = (f32[1,256,128]{2,0,1:T(1,128)S(1)}, f32[1,256,128]{2,0,1:T(1,128)S(1)}, u32[]{:S(2)}, u32[]{:S(2)}) collective-permute-start(f32[1,256,128]{2,0,1:T(1,128)S(1)} %get-tuple-element.25), channel_id=1, source_target_pairs={{0,12},{2,14},{4,8},{6,10},{8,4},{10,6},{12,0},{14,2},{1,13},{3,15... | collective-permute-start | bytes 393224 | tf_op jit(solution)/shard_map/ppermute | solution.py:21
  56.2 14.7 %collective-permute-start.6 = (f32[1,256,128]{2,0,1:T(1,128)S(1)}, f32[1,256,128]{2,0,1:T(1,128)S(1)}, u32[]{:S(2)}, u32[]{:S(2)}) collective-permute-start(f32[1,256,128]{2,0,1:T(1,128)S(1)} %get-tuple-element.24), channel_id=1, source_target_pairs={{0,14},{2,12},{4,10},{6,8},{8,6},{10,4},{12,2},{14,0},{1,15},{3,13... | collective-permute-start | bytes 393224 | tf_op jit(solution)/shard_map/ppermute | solution.py:21
  86.7 33.5 %all-to-all-start.1 = ((f32[8,256,128]{2,1,0:T(8,128)}), f32[8,256,128]{2,1,0:T(8,128)}, u32[]{:S(2)}, u32[]{:S(2)}) async-start(f32[8,256,128]{2,1,0:T(8,128)} %bitcast.131), calls=%async_computation.1 | async-start | bytes 2097152 | tf_op jit(solution)/shard_map/all_to_all | solution.py:32
  120.2 4.5 %copy-start.10 = (f32[16,256,128]{1,2,0:T(8,128)S(1)}, f32[16,256,128]{1,2,0:T(8,128)}, u32[]{:S(2)}) copy-start(f32[16,256,128]{1,2,0:T(8,128)} %fusion.34) | copy-start | bytes 6291460
  120.2 4.5 %copy-start.12 = (bf16[16,128,128]{2,1,0:T(8,128)(2,1)S(1)}, bf16[16,128,128]{2,1,0:T(8,128)(2,1)}, u32[]{:S(2)}) copy-start(bf16[16,128,128]{2,1,0:T(8,128)(2,1)} %copy-done.11) | copy-start | bytes 1572868
  124.3 10.1 %collective-permute-start.7 = (f32[1,256,128]{2,0,1:T(1,128)}, f32[1,256,128]{2,0,1:T(1,128)}, u32[]{:S(2)}, u32[]{:S(2)}) collective-permute-start(f32[1,256,128]{2,0,1:T(1,128)} %get-tuple-element.22), channel_id=1, source_target_pairs={{0,2},{2,0},{4,6},{6,4},{8,10},{10,8},{12,14},{14,12},{1,3},{3,1},... | collective-permute-start | bytes 393224 | tf_op jit(solution)/shard_map/ppermute | solution.py:21
  126.1 5.4 %copy-start.15 = (f32[1,256,128]{2,0,1:T(1,128)S(1)}, f32[1,256,128]{2,0,1:T(1,128)}, u32[]{:S(2)}) copy-start(f32[1,256,128]{2,0,1:T(1,128)} %get-tuple-element.19) | copy-start | bytes 393220
  126.1 5.4 %copy-start.14 = (f32[1,256,128]{2,0,1:T(1,128)S(1)}, f32[1,256,128]{2,0,1:T(1,128)}, u32[]{:S(2)}) copy-start(f32[1,256,128]{2,0,1:T(1,128)} %get-tuple-element.18) | copy-start | bytes 393220
  128.4 24.3 %copy-start.5 = (f32[16,128,128]{1,2,0:T(8,128)S(1)}, f32[16,128,128]{1,2,0:T(8,128)}, u32[]{:S(2)}) copy-start(f32[16,128,128]{1,2,0:T(8,128)} %fusion.36) | copy-start | bytes 3145732
  128.4 8.5 %collective-permute-start.8 = (f32[1,256,128]{2,0,1:T(1,128)S(1)}, f32[1,256,128]{2,0,1:T(1,128)S(1)}, u32[]{:S(2)}, u32[]{:S(2)}) collective-permute-start(f32[1,256,128]{2,0,1:T(1,128)S(1)} %copy-done.17), channel_id=1, source_target_pairs={{0,4},{2,6},{4,0},{6,2},{8,12},{10,14},{12,8},{14,10},{1,5},{3,7},... | collective-permute-start | bytes 393224 | tf_op jit(solution)/shard_map/ppermute | solution.py:21
  128.5 11.9 %collective-permute-start.9 = (f32[1,256,128]{2,0,1:T(1,128)S(1)}, f32[1,256,128]{2,0,1:T(1,128)S(1)}, u32[]{:S(2)}, u32[]{:S(2)}) collective-permute-start(f32[1,256,128]{2,0,1:T(1,128)S(1)} %copy-done.16), channel_id=1, source_target_pairs={{0,6},{2,4},{4,2},{6,0},{8,14},{10,12},{12,10},{14,8},{1,7},{3,5},... | collective-permute-start | bytes 393224 | tf_op jit(solution)/shard_map/ppermute | solution.py:21
  131.5 18.2 %collective-permute-start.10 = (f32[1,256,128]{2,0,1:T(1,128)S(1)}, f32[1,256,128]{2,0,1:T(1,128)S(1)}, u32[]{:S(2)}, u32[]{:S(2)}) collective-permute-start(f32[1,256,128]{2,0,1:T(1,128)S(1)} %copy-done.15), channel_id=1, source_target_pairs={{0,8},{2,10},{4,12},{6,14},{8,0},{10,2},{12,4},{14,6},{1,9},{3,11}... | collective-permute-start | bytes 393224 | tf_op jit(solution)/shard_map/ppermute | solution.py:21
  131.5 21.2 %collective-permute-start.11 = (f32[1,256,128]{2,0,1:T(1,128)S(1)}, f32[1,256,128]{2,0,1:T(1,128)S(1)}, u32[]{:S(2)}, u32[]{:S(2)}) collective-permute-start(f32[1,256,128]{2,0,1:T(1,128)S(1)} %copy-done.14), channel_id=1, source_target_pairs={{0,10},{2,8},{4,14},{6,12},{8,2},{10,0},{12,6},{14,4},{1,11},{3,9}... | collective-permute-start | bytes 393224 | tf_op jit(solution)/shard_map/ppermute | solution.py:21
  134.4 18.3 %collective-permute-start.12 = (f32[1,256,128]{2,0,1:T(1,128)S(1)}, f32[1,256,128]{2,0,1:T(1,128)S(1)}, u32[]{:S(2)}, u32[]{:S(2)}) collective-permute-start(f32[1,256,128]{2,0,1:T(1,128)S(1)} %get-tuple-element.17), channel_id=1, source_target_pairs={{0,12},{2,14},{4,8},{6,10},{8,4},{10,6},{12,0},{14,2},{1,13},{3,15... | collective-permute-start | bytes 393224 | tf_op jit(solution)/shard_map/ppermute | solution.py:21
  136.9 15.8 %collective-permute-start.13 = (f32[1,256,128]{2,0,1:T(1,128)S(1)}, f32[1,256,128]{2,0,1:T(1,128)S(1)}, u32[]{:S(2)}, u32[]{:S(2)}) collective-permute-start(f32[1,256,128]{2,0,1:T(1,128)S(1)} %get-tuple-element.16), channel_id=1, source_target_pairs={{0,14},{2,12},{4,10},{6,8},{8,6},{10,4},{12,2},{14,0},{1,15},{3,13... | collective-permute-start | bytes 393224 | tf_op jit(solution)/shard_map/ppermute | solution.py:21
  (12 other events, 24.1 us)
